TPU v7x, 32 devices: a whole 2x2x4 slice. The times are simulated.
32 devices in a mesh: dp: 16 (over z, x, core), seq: 2 (over y).
Axes of the slice: x: 2, y: 2, z: 4, core: 2. Of those that a mesh axis runs over, the one named last changes fastest.
Arguments:
- inputs: bfloat16 [2, 16, 256, 768], P(None, 'dp', 'seq'), may hold values from -6 to 6
- cotangent: bfloat16 [2, 16, 256, 768], P(None, 'dp', 'seq'), may hold values from -6 to 6
- w_qkv: float32 [1769472], P(('dp', 'seq')), may hold values from -0.21875 to 0.21875
- w_out: float32 [589824], P(('dp', 'seq')), may hold values from -0.21875 to 0.21875
- w_fc1: float32 [2359296], P(('dp', 'seq')), may hold values from -0.21875 to 0.21875
- w_fc2: float32 [2359296], P(('dp', 'seq')), may hold values from -0.109375 to 0.109375
- vectors: float32 [11520], P(('dp', 'seq')), may hold values from -0.9 to 1.5, as said below
- offsets: int32 [3, 12], replicated, may hold values from 0 to 3, as said below
Outputs:
- layer_out: bfloat16 [2, 16, 256, 768], P(None, 'dp', 'seq')
- input_grad: float32 [2, 16, 256, 768], P(None, 'dp', 'seq')
- grad_qkv: float32 [1769472], P(('dp', 'seq'))
- grad_out: float32 [589824], P(('dp', 'seq'))
- grad_fc1: float32 [2359296], P(('dp', 'seq'))
- grad_fc2: float32 [2359296], P(('dp', 'seq'))
- grad_vectors: float32 [11520], P(('dp', 'seq'))
Inputs may be any that keep to these rules, and one draw needn't show every extreme that they name: `offsets`: row b (b = 0, 1, 2) holds every head's offset below the dilation 1, 2, 4 of branch b; each value below a branch's dilation is held by 12 divided by that dilation heads. `vectors`: the four gains lie in 0.5 to 1.5; the biases lie in -0.9 to 0.9.
All inputs are finite; a program needn't handle non-finite values.
Results may differ from a plain program's by a relative error of at most 0.012.
The roundings to bfloat16 on the way count: a program that leaves them out, or rounds other values in their place, can miss the bound.
Values may be sent and summed in bfloat16 or wider, within the bound.
A program may use at most 192 MiB of HBM per device.

v0:
```python
from functools import partial

import jax
import jax.numpy as jnp
from jax import lax
from jax.sharding import PartitionSpec as P

D = 768
HEADS = 12
FF = 3072
HEAD_DIM = 64
TOK_BLK = 128
MB = 2


EPSILON = 1e-05
NEGATIVE = -1e30
DILATIONS = (1, 2, 4)


def layer_norm(features, gain_vec):
    row_mean = jnp.mean(features, axis=-1, keepdims=True)
    centred = features - row_mean
    row_var = jnp.mean(centred * centred, axis=-1, keepdims=True)
    return centred * lax.rsqrt(row_var + EPSILON) * gain_vec


def norm_back(features, gain_vec, grad_normed):
    normed_out, pullback = jax.vjp(layer_norm, features, gain_vec)
    return pullback(grad_normed)


def matmul(left_op, right_op):
    return jnp.dot(left_op, right_op, preferred_element_type=jnp.float32)


def outer_sum(left_op, right_op):
    return lax.dot_general(
        left_op, right_op, (((0,), (0,)), ((), ())), preferred_element_type=jnp.float32
    )


def inner_back(left_op, right_op):
    return lax.dot_general(
        left_op, right_op, (((1,), (1,)), ((), ())), preferred_element_type=jnp.float32
    )


def split_vectors(vectors, model_width, ffn_width):
    piece_sizes = (model_width,) * 6 + (ffn_width, ffn_width, model_width)
    pieces = []
    position = 0
    for piece_len in piece_sizes:
        pieces.append(vectors[position : position + piece_len])
        position = position + piece_len
    return pieces


def head_masks(offsets, branch, head_size):
    dilate = DILATIONS[branch]
    chosen = jnp.arange(dilate, dtype=jnp.int32)[:, None] == offsets[branch][None, :]
    return (chosen, jnp.repeat(chosen, head_size, axis=1))


def select_rows(dense_rows, chosen):
    dilate = chosen.shape[0]
    folded = dense_rows.reshape(dense_rows.shape[0] // dilate, dilate, dense_rows.shape[1])
    picked = jnp.where(chosen[None], folded, jnp.zeros((), dense_rows.dtype))
    return jnp.sum(picked, axis=1, dtype=dense_rows.dtype)


def spread_rows(sparse_rows, chosen, filler):
    dilate = chosen.shape[0]
    spread = jnp.where(chosen[None], sparse_rows[:, None, :], filler)
    return spread.reshape(sparse_rows.shape[0] * dilate, sparse_rows.shape[1])


def window_mask(query_rows, key_rows, first_row, key_first, seg_rows):
    row_ids = first_row + jnp.arange(query_rows, dtype=jnp.int32)[:, None]
    col_ids = key_first + jnp.arange(key_rows, dtype=jnp.int32)[None, :]
    return (col_ids <= row_ids) & (col_ids >= 0) & (col_ids // seg_rows == row_ids // seg_rows)


def masked_scores(queries, keys_win, allowed, score_scale):
    query_heads = queries.reshape(queries.shape[0], HEADS, -1)
    key_heads = keys_win.reshape(keys_win.shape[0], HEADS, -1)
    scores = (
        jnp.einsum("qhd,khd->hqk", query_heads, key_heads, preferred_element_type=jnp.float32)
        * score_scale
    )
    return jnp.where(allowed[None], scores, NEGATIVE)


def attend_piece(queries, keys_win, values_win, allowed, score_scale):
    scores = masked_scores(queries, keys_win, allowed, score_scale)
    log_sums = jax.nn.logsumexp(scores, axis=2)
    weights_low = jnp.exp(scores - log_sums[:, :, None]).astype(jnp.bfloat16)
    value_heads = values_win.reshape(values_win.shape[0], HEADS, -1)
    result = jnp.einsum(
        "hqk,khd->qhd", weights_low, value_heads, preferred_element_type=jnp.float32
    )
    return (result.reshape(queries.shape[0], -1), log_sums)


def attend(queries, keys_win, values_win, first_row, key_first, seg_rows, score_scale):
    rows = queries.shape[0]
    allowed = window_mask(rows, keys_win.shape[0], first_row + 0, key_first, seg_rows)
    result, log_sums = attend_piece(queries, keys_win, values_win, allowed, score_scale)
    return (result, log_sums)


def back_piece(
    queries, keys_win, values_win, log_sums, grad_result, grad_log, allowed, score_scale
):
    query_rows = queries.shape[0]
    scores = masked_scores(queries, keys_win, allowed, score_scale)
    probability = jnp.exp(scores - log_sums[:, :, None])
    query_heads = queries.reshape(query_rows, HEADS, -1)
    key_heads = keys_win.reshape(keys_win.shape[0], HEADS, -1)
    value_heads = values_win.reshape(values_win.shape[0], HEADS, -1)
    grad_heads = grad_result.reshape(query_rows, HEADS, -1)
    grad_probs = jnp.einsum(
        "qhd,khd->hqk", grad_heads, value_heads, preferred_element_type=jnp.float32
    )
    row_dot = jnp.sum(probability * grad_probs, axis=2, keepdims=True)
    grad_scores = (probability * (grad_probs - row_dot + grad_log.T[:, :, None])).astype(
        jnp.bfloat16
    )
    grad_query = (
        jnp.einsum("hqk,khd->qhd", grad_scores, key_heads, preferred_element_type=jnp.float32)
        * score_scale
    )
    grad_keys = (
        jnp.einsum("hqk,qhd->khd", grad_scores, query_heads, preferred_element_type=jnp.float32)
        * score_scale
    )
    grad_values = jnp.einsum(
        "hqk,qhd->khd",
        probability.astype(jnp.bfloat16),
        grad_heads,
        preferred_element_type=jnp.float32,
    )
    key_rows = keys_win.shape[0]
    return (
        grad_query.reshape(query_rows, -1),
        grad_keys.reshape(key_rows, -1),
        grad_values.reshape(key_rows, -1),
    )


def attend_back(
    queries,
    keys_win,
    values_win,
    log_sums,
    grad_result,
    grad_log,
    first_row,
    key_first,
    seg_rows,
    score_scale,
):
    rows = queries.shape[0]
    allowed = window_mask(rows, keys_win.shape[0], first_row + 0, key_first, seg_rows)
    query_part, key_part, value_part = back_piece(
        queries, keys_win, values_win, log_sums, grad_result, grad_log, allowed, score_scale
    )
    return (query_part, key_part, value_part)


def per_device(inputs, cotangent, w_qkv, w_out, w_fc1, w_fc2, vectors, offsets):
    seq_count = lax.axis_size("seq")
    seq_index = lax.axis_index("seq")
    seq_len = TOK_BLK * seq_count
    seg_rows = seq_len // 4
    score_scale = HEAD_DIM ** (-0.5)
    shards = (
        w_qkv.astype(jnp.bfloat16),
        w_out.astype(jnp.bfloat16),
        w_fc1.astype(jnp.bfloat16),
        w_fc2.astype(jnp.bfloat16),
        vectors.astype(jnp.bfloat16),
    )

    def unpack(gathered):
        qkv_flat, out_flat, up_flat, down_flat, vector_flat = gathered
        return (
            qkv_flat.reshape(D, 3 * D),
            out_flat.reshape(D, D),
            up_flat.reshape(D, FF),
            down_flat.reshape(FF, D),
            vector_flat.astype(jnp.float32),
        )

    selectors = [head_masks(offsets, branch, HEAD_DIM) for branch in range(3)]
    plans = []
    for branch in range(3):
        block_rows = TOK_BLK // DILATIONS[branch]
        window = max(seg_rows, block_rows)
        first_row = seq_index * block_rows
        plans.append((first_row, block_rows, window, first_row + block_rows - window))
    totals = None
    layer_rows = []
    grad_rows = []
    for micro_batch in range(MB):
        params = unpack(
            (
                lax.all_gather(shards[0], ("dp", "seq"), axis=0, tiled=True),
                lax.all_gather(shards[1], ("dp", "seq"), axis=0, tiled=True),
                lax.all_gather(shards[2], ("dp", "seq"), axis=0, tiled=True),
                lax.all_gather(shards[3], ("dp", "seq"), axis=0, tiled=True),
                lax.all_gather(shards[4], ("dp", "seq"), axis=0, tiled=True),
            )
        )
        qkv_weight, out_weight, up_weight, down_weight, vector_vals = params
        (
            gain_in,
            bias_query,
            bias_value,
            gain_attn,
            bias_out,
            gain_mid,
            bias_up,
            gain_ffn,
            bias_down,
        ) = split_vectors(vector_vals, D, FF)
        tokens = inputs[micro_batch, 0].astype(jnp.float32)
        normed = layer_norm(tokens, gain_in).astype(jnp.bfloat16)
        bias_full = jnp.concatenate([bias_query, jnp.zeros_like(bias_query), bias_value])
        qkv_rows = (matmul(normed, qkv_weight) + bias_full).astype(jnp.bfloat16)
        sparse_query = [select_rows(qkv_rows[:, :D], selectors[branch][1]) for branch in range(3)]
        sparse_keys = [
            select_rows(qkv_rows[:, D : 2 * D], selectors[branch][1]) for branch in range(3)
        ]
        sparse_values = [
            select_rows(qkv_rows[:, 2 * D :], selectors[branch][1]) for branch in range(3)
        ]
        windows = []
        gathered = (
            lax.all_gather(sparse_keys[0], "seq", axis=0, tiled=True),
            lax.all_gather(sparse_values[0], "seq", axis=0, tiled=True),
            lax.all_gather(sparse_keys[1], "seq", axis=0, tiled=True),
            lax.all_gather(sparse_values[1], "seq", axis=0, tiled=True),
            lax.all_gather(sparse_keys[2], "seq", axis=0, tiled=True),
            lax.all_gather(sparse_values[2], "seq", axis=0, tiled=True),
        )
        for branch in range(3):
            first_row, block_rows, window, start = plans[branch]
            begin = jnp.maximum(start, 0)
            windows.append(
                (
                    lax.dynamic_slice_in_dim(gathered[2 * branch], begin, window, 0),
                    lax.dynamic_slice_in_dim(gathered[2 * branch + 1], begin, window, 0),
                    begin,
                )
            )
        branch_outs = []
        branch_logs = []
        sparse_logs = []
        for branch in range(3):
            keys_win, values_win, key_first = windows[branch]
            result, log_sums = attend(
                sparse_query[branch],
                keys_win,
                values_win,
                plans[branch][0],
                key_first,
                seg_rows,
                score_scale,
            )
            sparse_logs.append(log_sums)
            branch_outs.append(
                spread_rows(result, selectors[branch][1], 0.0).reshape(TOK_BLK, HEADS, HEAD_DIM)
            )
            branch_logs.append(spread_rows(log_sums.T, selectors[branch][0], NEGATIVE))
        stacked = jnp.stack(branch_logs)
        total_log = jax.nn.logsumexp(stacked, axis=0)
        mixing = jnp.exp(stacked - total_log[None])
        mixed = sum(
            (mixing[branch][:, :, None] * branch_outs[branch] for branch in range(3))
        ).reshape(TOK_BLK, D)
        inner = layer_norm(mixed, gain_attn).astype(jnp.bfloat16)
        middle = tokens + (matmul(inner, out_weight) + bias_out)
        normed_mid = layer_norm(middle, gain_mid).astype(jnp.bfloat16)
        hidden = matmul(normed_mid, up_weight) + bias_up
        active, gelu_back = jax.vjp(partial(jax.nn.gelu, approximate=False), hidden)
        inner_ffn = layer_norm(active, gain_ffn).astype(jnp.bfloat16)
        layer_rows.append(
            (middle + (matmul(inner_ffn, down_weight) + bias_down)).astype(jnp.bfloat16)
        )
        back_params = unpack(
            (
                lax.all_gather(shards[0], ("dp", "seq"), axis=0, tiled=True),
                lax.all_gather(shards[1], ("dp", "seq"), axis=0, tiled=True),
                lax.all_gather(shards[2], ("dp", "seq"), axis=0, tiled=True),
                lax.all_gather(shards[3], ("dp", "seq"), axis=0, tiled=True),
                lax.all_gather(shards[4], ("dp", "seq"), axis=0, tiled=True),
            )
        )
        qkv_weight, out_weight, up_weight, down_weight = (
            back_params[0],
            back_params[1],
            back_params[2],
            back_params[3],
        )
        grad_layer = cotangent[micro_batch, 0].astype(jnp.float32)
        grad_down = grad_layer.astype(jnp.bfloat16)
        grad_inner_ffn = inner_back(grad_down, down_weight)
        grad_active, grad_gain_ffn = norm_back(active, gain_ffn, grad_inner_ffn)
        grad_hidden = gelu_back(grad_active)[0].astype(jnp.bfloat16)
        grad_normed_mid = inner_back(grad_hidden, up_weight)
        grad_middle_part, grad_gain_mid = norm_back(middle, gain_mid, grad_normed_mid)
        grad_middle = grad_layer + grad_middle_part
        grad_branch = grad_middle.astype(jnp.bfloat16)
        grad_inner = inner_back(grad_branch, out_weight)
        grad_mixed, grad_gain_attn = norm_back(mixed, gain_attn, grad_inner)
        grad_heads = grad_mixed.reshape(TOK_BLK, HEADS, HEAD_DIM)
        along_out = [jnp.sum(grad_heads * branch_outs[branch], axis=2) for branch in range(3)]
        common = sum((mixing[branch] * along_out[branch] for branch in range(3)))
        grad_query_dense = jnp.zeros((TOK_BLK, D), jnp.float32)
        key_terms = []
        for branch in range(3):
            chosen, wide_mask = selectors[branch]
            keys_win, values_win, key_first = windows[branch]
            grad_result = select_rows(
                (mixing[branch][:, :, None] * grad_heads).reshape(TOK_BLK, D), wide_mask
            ).astype(jnp.bfloat16)
            grad_log = select_rows(mixing[branch] * (along_out[branch] - common), chosen)
            query_part, key_part, value_part = attend_back(
                sparse_query[branch],
                keys_win,
                values_win,
                sparse_logs[branch],
                grad_result,
                grad_log,
                plans[branch][0],
                key_first,
                seg_rows,
                score_scale,
            )
            grad_query_dense = grad_query_dense + spread_rows(query_part, wide_mask, 0.0)
            key_terms.append(key_part)
            key_terms.append(value_part)
        full_terms = []
        for branch in range(3):
            full_rows = seq_len // DILATIONS[branch]
            for member in range(2):
                empty = jnp.zeros((full_rows, D), jnp.float32)
                full_terms.append(
                    lax.dynamic_update_slice_in_dim(
                        empty, key_terms[2 * branch + member], windows[branch][2], 0
                    )
                )
        owned_keys = (
            lax.psum_scatter(
                full_terms[0].astype(jnp.bfloat16), "seq", scatter_dimension=0, tiled=True
            ).astype(jnp.float32),
            lax.psum_scatter(
                full_terms[1].astype(jnp.bfloat16), "seq", scatter_dimension=0, tiled=True
            ).astype(jnp.float32),
            lax.psum_scatter(
                full_terms[2].astype(jnp.bfloat16), "seq", scatter_dimension=0, tiled=True
            ).astype(jnp.float32),
            lax.psum_scatter(
                full_terms[3].astype(jnp.bfloat16), "seq", scatter_dimension=0, tiled=True
            ).astype(jnp.float32),
            lax.psum_scatter(
                full_terms[4].astype(jnp.bfloat16), "seq", scatter_dimension=0, tiled=True
            ).astype(jnp.float32),
            lax.psum_scatter(
                full_terms[5].astype(jnp.bfloat16), "seq", scatter_dimension=0, tiled=True
            ).astype(jnp.float32),
        )
        grad_keys_dense = sum(
            (spread_rows(owned_keys[2 * branch], selectors[branch][1], 0.0) for branch in range(3))
        )
        grad_values_dense = sum(
            (
                spread_rows(owned_keys[2 * branch + 1], selectors[branch][1], 0.0)
                for branch in range(3)
            )
        )
        grad_qkv_rows = jnp.concatenate(
            [grad_query_dense, grad_keys_dense, grad_values_dense], axis=1
        ).astype(jnp.bfloat16)
        grad_bias_query = jnp.sum(grad_qkv_rows[:, :D].astype(jnp.float32), axis=0)
        grad_bias_value = jnp.sum(grad_qkv_rows[:, 2 * D :].astype(jnp.float32), axis=0)
        grad_normed = inner_back(grad_qkv_rows, qkv_weight)
        grad_input_part, grad_gain_in = norm_back(tokens, gain_in, grad_normed)
        grad_rows.append(grad_middle + grad_input_part)
        vector_grad = jnp.concatenate(
            [
                grad_gain_in,
                grad_bias_query,
                grad_bias_value,
                grad_gain_attn,
                jnp.sum(grad_branch.astype(jnp.float32), axis=0),
                grad_gain_mid,
                jnp.sum(grad_hidden.astype(jnp.float32), axis=0),
                grad_gain_ffn,
                jnp.sum(grad_down.astype(jnp.float32), axis=0),
            ]
        )
        micro_grads = (
            outer_sum(normed, grad_qkv_rows),
            outer_sum(inner, grad_branch),
            outer_sum(normed_mid, grad_hidden),
            outer_sum(inner_ffn, grad_down),
            vector_grad,
        )
        if totals is None:
            totals = micro_grads
        else:
            totals = tuple(
                (total_sum + grad_one for total_sum, grad_one in zip(totals, micro_grads))
            )
    owned_grads = (
        lax.psum_scatter(totals[0].reshape(-1), ("dp", "seq"), scatter_dimension=0, tiled=True),
        lax.psum_scatter(totals[1].reshape(-1), ("dp", "seq"), scatter_dimension=0, tiled=True),
        lax.psum_scatter(totals[2].reshape(-1), ("dp", "seq"), scatter_dimension=0, tiled=True),
        lax.psum_scatter(totals[3].reshape(-1), ("dp", "seq"), scatter_dimension=0, tiled=True),
        lax.psum_scatter(totals[4], ("dp", "seq"), scatter_dimension=0, tiled=True),
    )
    layer_out = jnp.stack(layer_rows)[:, None]
    input_grad = jnp.stack(grad_rows)[:, None]
    return (
        layer_out,
        input_grad,
        owned_grads[0],
        owned_grads[1],
        owned_grads[2],
        owned_grads[3],
        owned_grads[4],
    )


def solution(mesh):
    return jax.shard_map(
        per_device,
        mesh=mesh,
        in_specs=(
            P(None, "dp", "seq", None),
            P(None, "dp", "seq", None),
            P(("dp", "seq")),
            P(("dp", "seq")),
            P(("dp", "seq")),
            P(("dp", "seq")),
            P(("dp", "seq")),
            P(),
        ),
        out_specs=(
            P(None, "dp", "seq", None),
            P(None, "dp", "seq", None),
            P(("dp", "seq")),
            P(("dp", "seq")),
            P(("dp", "seq")),
            P(("dp", "seq")),
            P(("dp", "seq")),
        ),
        check_vma=False,
    )
```

profile of v0, /device:TPU:0, one launch (start us, length us, event | category | flops | bytes accessed | tf_op | source)
XLA Modules:
  0.0 1087.3 jit_solution(2737738455100650751)
XLA Ops:
  14.5 42.2 %all-reduce = bf16[11520]{0:T(1024)(128)(2,1)S(1)} all-reduce(bf16[11520]{0:T(1024)(128)(2,1)S(1)} %dynamic-update-slice), channel_id=1, replica_groups=mesh['dp'=16,'seq'=2] {'dp','seq'}, use_global_device_ids=true, to_apply=%add | all-reduce | flops 11520 | bytes 46080
  71.8 59.2 %all-gather.5.cloned.1.call-done = bf16[1769472]{0:T(1024)(128)(2,1)} async-done(((bf16[55296]{0:T(1024)(128)(2,1)}), bf16[1769472]{0:T(1024)(128)(2,1)}) %all-gather.5.cloned.1.call-update) | async-done | bytes 3538960 | tf_op jit(solution)/shard_map/all_gather | solution.py:208
  131.0 6.3 reshape.1622
  144.1 4.8 all_gather.68
  150.2 4.8 all_gather.77
  159.6 5.9 all_gather.67
  167.1 5.3 all_gather.76
  173.7 10.0 all_gather.69
  184.3 5.8 all_gather.71
  190.1 4.8 all_gather.80
  195.2 5.4 all_gather.70
  200.8 5.5 all_gather.79
  212.4 7.4 all_gather.66
  220.1 8.1 all_gather.75
  228.4 7.1 all_gather.78
  277.3 8.4 reshape.1639
  285.8 8.2 fusion.304
  294.5 5.4 fusion.302
  300.5 9.4 reshape.1640
  309.9 4.3 multiply_reduce_fusion.3
  456.6 6.4 fusion.295
  482.4 4.0 convolution_add_fusion.6
  497.1 6.1 fusion.161
  513.8 9.3 add_bitcast_fusion
  545.9 9.0 convolution_add_fusion.1
  564.7 10.8 reshape.1675
  575.5 9.6 copy.815
  625.6 3.8 convert_reduce_fusion.8
  630.8 4.1 convolution_add_fusion
  634.9 8.2 reshape.1672
  655.0 39.2 %all-reduce.5 = f32[11520]{0:T(1024)S(1)} all-reduce(f32[11520]{0:T(1024)S(1)} %add.758), channel_id=18, replica_groups=mesh['dp'=16,'seq'=2] {'dp','seq'}, use_global_device_ids=true, to_apply=%region_112.113.clone | all-reduce | flops 11520 | bytes 92160
  696.1 377.7 %all-reduce.9.cloned.1.call-done = (f32[1769472]{0:T(1024)}, f32[589824]{0:T(1024)}, f32[2359296]{0:T(1024)}, f32[2359296]{0:T(1024)}) async-done(((f32[1769472]{0:T(1024)}, f32[589824]{0:T(1024)}, f32[2359296]{0:T(1024)}, f32[2359296]{0:T(1024)}), (f32[1769472]{0:T(1024)}, f32[589824]{0:T(1024)}, f32[2359296]{0:T(1024)}, f32[2359296]{0:T(1024)})) %all-reduce.9.cloned.1.call-update) | async-done | bytes 28311568
  (882 shorter events, 362.8 us)
Async XLA Ops:
  7.2 50.8 %copy-start.6 = (bf16[2,1,128,768]{3,2,1,0:T(8,128)(2,1)S(1)}, bf16[2,1,128,768]{3,2,1,0:T(8,128)(2,1)}, u32[]{:S(2)}) copy-start(bf16[2,1,128,768]{3,2,1,0:T(8,128)(2,1)} %param.8) | copy-start | bytes 1179652
  7.2 61.2 %all-gather.7.cloned.1.call-start = ((), (), s32[]{:S(2)}) async-start(), calls=%async_computation.13 | async-start | bytes 1216512 | tf_op jit(solution)/shard_map/all_gather | solution.py:209
  8.8 122.2 %all-gather.5.cloned.1.call-start = ((), (), s32[]{:S(2)}) async-start(), calls=%async_computation.12 | async-start | bytes 3649536 | tf_op jit(solution)/shard_map/all_gather | solution.py:208
  10.5 266.8 %all-gather.9.cloned.1.call-start = ((), (), s32[]{:S(2)}) async-start(), calls=%async_computation.14 | async-start | bytes 4866048 | tf_op jit(solution)/shard_map/all_gather | solution.py:210
  12.2 288.3 %all-gather.11.cloned.1.call-start = ((), (), s32[]{:S(2)}) async-start(), calls=%async_computation.15 | async-start | bytes 4866048 | tf_op jit(solution)/shard_map/all_gather | solution.py:211
  13.9 571.2 %reduce-scatter.37.cloned.1.call-start = ((), (), s32[]{:S(2)}) async-start(), calls=%async_computation.26 | async-start | bytes 147456 | tf_op jit(solution)/shard_map/reduce_scatter | solution.py:370
  14.1 57.7 %copy-start.177 = (pred[12]{0:T(512)(128)(4,1)}, pred[12]{0:T(512)(128)(4,1)S(1)}, u32[]{:S(2)}) copy-start(pred[12]{0:T(512)(128)(4,1)S(1)} %compare_bitcast_fusion) | copy-start | bytes 40
  149.3 57.3 %copy-start.35 = (f32[12,32,64]{2,1,0:T(8,128)}, f32[12,32,64]{2,1,0:T(8,128)S(1)}, u32[]{:S(2)}) copy-start(f32[12,32,64]{2,1,0:T(8,128)S(1)} %get-tuple-element.247) | copy-start | bytes 294916
  149.6 57.1 %copy-start.107 = (f32[12,32]{1,0:T(8,128)}, f32[12,32]{1,0:T(8,128)S(1)}, u32[]{:S(2)}) copy-start(f32[12,32]{1,0:T(8,128)S(1)} %fusion.263) | copy-start | bytes 4612
  155.7 55.6 %copy-start.34 = (f32[12,32,64]{2,1,0:T(8,128)}, f32[12,32,64]{2,1,0:T(8,128)S(1)}, u32[]{:S(2)}) copy-start(f32[12,32,64]{2,1,0:T(8,128)S(1)} %get-tuple-element.249) | copy-start | bytes 294916
  155.9 55.3 %copy-start.106 = (f32[12,32]{1,0:T(8,128)}, f32[12,32]{1,0:T(8,128)S(1)}, u32[]{:S(2)}) copy-start(f32[12,32]{1,0:T(8,128)S(1)} %fusion.266) | copy-start | bytes 4612
  166.2 69.4 %copy-start.23 = (f32[12,64,64]{1,2,0:T(8,128)}, f32[12,64,64]{1,2,0:T(8,128)S(1)}, u32[]{:S(2)}) copy-start(f32[12,64,64]{1,2,0:T(8,128)S(1)} %get-tuple-element.251) | copy-start | bytes 589828
  166.3 69.2 %copy-start.105 = (f32[12,64]{1,0:T(8,128)}, f32[12,64]{1,0:T(8,128)S(1)}, u32[]{:S(2)}) copy-start(f32[12,64]{1,0:T(8,128)S(1)} %fusion.262) | copy-start | bytes 9220
  173.0 63.1 %copy-start.24 = (f32[12,64,64]{1,2,0:T(8,128)}, f32[12,64,64]{1,2,0:T(8,128)S(1)}, u32[]{:S(2)}) copy-start(f32[12,64,64]{1,2,0:T(8,128)S(1)} %get-tuple-element.253) | copy-start | bytes 589828
  173.1 62.9 %copy-start.108 = (f32[12,64]{1,0:T(8,128)}, f32[12,64]{1,0:T(8,128)S(1)}, u32[]{:S(2)}) copy-start(f32[12,64]{1,0:T(8,128)S(1)} %fusion.265) | copy-start | bytes 9220
  183.9 73.7 %copy-start.32 = (bf16[128,768]{0,1:T(8,128)(2,1)}, bf16[128,768]{0,1:T(8,128)(2,1)S(1)}, u32[]{:S(2)}) copy-start(bf16[128,768]{0,1:T(8,128)(2,1)S(1)} %copy.643) | copy-start | bytes 589828
  184.1 53.5 %copy-start.58 = (bf16[128,768]{0,1:T(8,128)(2,1)}, bf16[128,768]{0,1:T(8,128)(2,1)S(1)}, u32[]{:S(2)}) copy-start(bf16[128,768]{0,1:T(8,128)(2,1)S(1)} %copy.631) | copy-start | bytes 589828
  184.2 52.9 %copy-start.59 = (bf16[128,768]{0,1:T(8,128)(2,1)}, bf16[128,768]{0,1:T(8,128)(2,1)S(1)}, u32[]{:S(2)}) copy-start(bf16[128,768]{0,1:T(8,128)(2,1)S(1)} %copy.652) | copy-start | bytes 589828
  382.1 204.4 %reduce-scatter.39.cloned.1.call-start = ((), (), s32[]{:S(2)}) async-start(), calls=%async_computation.27 | async-start | bytes 147456 | tf_op jit(solution)/shard_map/reduce_scatter | solution.py:370
  433.1 154.9 %reduce-scatter.31.cloned.1.call-start = ((), (), s32[]{:S(2)}) async-start(), calls=%async_computation.23 | async-start | bytes 147456 | tf_op jit(solution)/shard_map/reduce_scatter | solution.py:367
  437.9 151.6 %reduce-scatter.21.cloned.1.call-start = ((), (), s32[]{:S(2)}) async-start(), calls=%async_computation.18 | async-start | bytes 147456 | tf_op jit(solution)/shard_map/reduce_scatter | solution.py:367
  440.2 164.2 %reduce-scatter.25.cloned.1.call-start = ((), (), s32[]{:S(2)}) async-start(), calls=%async_computation.20 | async-start | bytes 294912 | tf_op jit(solution)/shard_map/reduce_scatter | solution.py:364
  442.5 163.5 %reduce-scatter.35.cloned.1.call-start = ((), (), s32[]{:S(2)}) async-start(), calls=%async_computation.25 | async-start | bytes 294912 | tf_op jit(solution)/shard_map/reduce_scatter | solution.py:364
  449.2 158.3 %reduce-scatter.19.cloned.1.call-start = ((), (), s32[]{:S(2)}) async-start(), calls=%async_computation.17 | async-start | bytes 294912 | tf_op jit(solution)/shard_map/reduce_scatter | solution.py:361
  463.1 146.1 %reduce-scatter.29.cloned.1.call-start = ((), (), s32[]{:S(2)}) async-start(), calls=%async_computation.22 | async-start | bytes 294912 | tf_op jit(solution)/shard_map/reduce_scatter | solution.py:361
  474.6 150.9 %reduce-scatter.33.cloned.1.call-start = ((), (), s32[]{:S(2)}) async-start(), calls=%async_computation.24 | async-start | bytes 589824 | tf_op jit(solution)/shard_map/reduce_scatter | solution.py:358
  486.4 139.2 %reduce-scatter.23.cloned.1.call-start = ((), (), s32[]{:S(2)}) async-start(), calls=%async_computation.19 | async-start | bytes 589824 | tf_op jit(solution)/shard_map/reduce_scatter | solution.py:358
  503.3 122.3 %reduce-scatter.17.cloned.1.call-start = ((), (), s32[]{:S(2)}) async-start(), calls=%async_computation.16 | async-start | bytes 589824 | tf_op jit(solution)/shard_map/reduce_scatter | solution.py:355
  523.2 102.4 %reduce-scatter.27.cloned.1.call-start = ((), (), s32[]{:S(2)}) async-start(), calls=%async_computation.21 | async-start | bytes 589824 | tf_op jit(solution)/shard_map/reduce_scatter | solution.py:355
  555.0 518.8 %all-reduce.9.cloned.1.call-start = ((), (), s32[]{:S(2)}) async-start(), calls=%async_computation.28 | async-start | bytes 56623104
  654.0 40.8 %copy-start.22 = (bf16[2,1,128,768]{3,2,1,0:T(8,128)(2,1)S(1)}, bf16[2,1,128,768]{3,2,1,0:T(8,128)(2,1)}, u32[]{:S(2)}) copy-start(bf16[2,1,128,768]{3,2,1,0:T(8,128)(2,1)} %param.9) | copy-start | bytes 1179652
  654.0 40.8 %copy-start.28 = (f32[128,768]{1,0:T(8,128)S(1)}, f32[128,768]{1,0:T(8,128)}, u32[]{:S(2)}) copy-start(f32[128,768]{1,0:T(8,128)} %copy-done.27) | copy-start | bytes 1179652
  (210 other events, 1153.7 us)
Sparse Core Ops, SparseCore 0:
  11.5 56.8 all-gather.6
  71.9 59.0 all-gather.4
  134.0 64.5 all-gather.8
  201.3 62.4 all-gather.10
  382.3 7.7 reduce-scatter.36
  433.2 7.7 reduce-scatter.38
  443.2 9.9 reduce-scatter.30
  455.4 9.9 reduce-scatter.20
  467.7 10.9 reduce-scatter.24
  480.8 10.9 reduce-scatter.34
  494.0 10.9 reduce-scatter.18
  507.1 10.9 reduce-scatter.28
  520.3 13.1 reduce-scatter.32
  535.7 13.1 reduce-scatter.22
  550.9 13.1 reduce-scatter.16
  566.3 13.1 reduce-scatter.26
  643.2 430.5 all-reduce.8
where the time goes:
time: 1100 us; the launch traced here: 1090 us
  waiting for transfers between devices  441 us (40%)
  local copies, waits for them, and re-layouts  242 us (22%)
  blocking collectives  156 us (14%)
  matrix products  152 us (14%)
  other arithmetic  78.2 us (7%)
  between operations  18.1 us (2%)
    unnamed x18, waiting for transfers between devices  378 us
    unnamed x2, blocking collectives  81.4 us
    all_gather x1, waiting for transfers between devices, per_device(): lax.all_gather(shards[0], ('dp', 'seq'), axis=0, tiled=True)  59.2 us
    dot_general x8, matrix products, outer_sum(): lax.dot_general(left_op, right_op, (((0,), (0,)), ((), ())), preferred_el...  43.4 us
    select_n x28, local copies, waits for them, and re-layouts, spread_rows(): spread = jnp.where(chosen[None], sparse_rows[:, None, :], filler)  37.1 us
    unnamed x480, local copies, waits for them, and re-layouts  24.9 us
    dot_general x8, matrix products, matmul(): return jnp.dot(left_op, right_op, preferred_element_type=jnp.float32)  24.1 us
  transfers between devices with their start and end apart: 17, of which 3 were waited for; matrix products, arithmetic and copies ran while one was open for 33% of the time, Pallas kernels for 0%

commit v1 on v0

--- a/solution.py
+++ b/solution.py
@@ -3,6 +3,8 @@
 import jax
 import jax.numpy as jnp
 from jax import lax
+from jax.experimental import pallas as pl
+from jax.experimental.pallas import tpu as pltpu
 from jax.sharding import PartitionSpec as P
 
 D = 768
@@ -11,6 +13,137 @@
 HEAD_DIM = 64
 TOK_BLK = 128
 MB = 2
+
+MESH = pl.DeviceIdType.MESH
+
+def coords():
+    dp = lax.axis_index("dp"); y = lax.axis_index("seq")
+    return dp // 4, (dp // 2) % 2, dp % 2, y
+
+def dev(z, x, c, y):
+    return (z * 4 + x * 2 + c, y)
+
+def slab(z, x, c, y):
+    return z * 8 + x * 4 + c * 2 + y
+
+def ag_body(nw, order, srcs, outs, send_sem, recv_sem, loc_sem):
+    z, x, c, y = coords()
+    barrier = pltpu.get_barrier_semaphore()
+    def sig(d):
+        pl.semaphore_signal(barrier, inc=1, device_id=d, device_id_type=MESH)
+    sig(dev(z, 1 - x, c, y)); sig(dev(z, x, 1 - c, y)); sig(dev(z, x, c, 1 - y))
+    @pl.when(z > 0)
+    def _(): sig(dev(z - 1, x, c, y))
+    @pl.when(z < 3)
+    def _(): sig(dev(z + 1, x, c, y))
+    pl.semaphore_wait(barrier, 3 + (z + 2) // 3 + (5 - z) // 3)
+
+    me = slab(z, x, c, y)
+    def cp(w, s, k, d):
+        own = outs[w].at[s]
+        return pltpu.make_async_remote_copy(src_ref=own, dst_ref=own,
+            send_sem=send_sem.at[w, k], recv_sem=recv_sem.at[w, s], device_id=d, device_id_type=MESH)
+    def waitr(w, s):
+        own = outs[w].at[s]
+        pltpu.make_async_remote_copy(src_ref=own, dst_ref=own,
+            send_sem=send_sem.at[w, 0], recv_sem=recv_sem.at[w, s], device_id=dev(z, 1 - x, c, y), device_id_type=MESH).wait_recv()
+    pend = []
+    def go(w, s, k, d, cond=None):
+        if cond is None:
+            cp(w, s, k, d).start()
+        else:
+            @pl.when(cond)
+            def _(): cp(w, s, k, d).start()
+        pend.append((w, s, k, d, cond))
+    xn, yn, cn = dev(z, 1 - x, c, y), dev(z, x, c, 1 - y), dev(z, x, 1 - c, y)
+    zr, zl = dev(lax.min(z + 1, 3), x, c, y), dev(lax.max(z - 1, 0), x, c, y)
+    def core(w, s, cond=None):
+        go(w, s, 8 + (s // 4) * 2 + s % 2, cn, cond)
+    def col(w, zz, right, left, cond=None):
+        s = slab(zz, x, c, y)
+        if right is not None: go(w, s, 24 + zz, zr, right)
+        if left is not None: go(w, s, 28 + zz, zl, left)
+        go(w, s, 0 + zz, xn, cond)
+        go(w, s, 4 + zz, yn, cond)
+        core(w, s, cond)
+    def own(w):
+        col(w, z, z < 3, z > 0)
+    def step(w, d):
+        cl = z - d >= 0
+        @pl.when(cl)
+        def _(): waitr(w, slab(z - d, x, c, y))
+        col(w, lax.max(z - d, 0), (z - d >= 0) & (z < 3), None, cl)
+        cr = z + d <= 3
+        @pl.when(cr)
+        def _(): waitr(w, slab(z + d, x, c, y))
+        col(w, lax.min(z + d, 3), None, (z + d <= 3) & (z > 0), cr)
+    def plane(w, zz, cond=None):
+        par = zz % 2
+        s = slab(zz, x + (1 - par) * (1 - 2 * x), c, y + par * (1 - 2 * y))
+        tgt = dev(z, x + par * (1 - 2 * x), c, y + (1 - par) * (1 - 2 * y))
+        def f():
+            waitr(w, s)
+        if cond is None: f()
+        else: pl.when(cond)(f)
+        go(w, s, 32 + zz, tgt, cond)
+        core(w, s, cond)
+    def plane2(w, zz, cond=None):
+        par = zz % 2
+        for s in (slab(zz, x + par * (1 - 2 * x), c, y + (1 - par) * (1 - 2 * y)), slab(zz, 1 - x, c, 1 - y)):
+            def f():
+                waitr(w, s)
+            if cond is None: f()
+            else: pl.when(cond)(f)
+            core(w, s, cond)
+    for w in range(nw):
+        pltpu.make_async_copy(srcs[w], outs[w].at[me], loc_sem.at[w]).start()
+    def both(fn, w, d):
+        if d == 0: fn(w, z)
+        else:
+            fn(w, lax.max(z - d, 0), z - d >= 0)
+            fn(w, lax.min(z + d, 3), z + d <= 3)
+    stages = []
+    def st(w, k):
+        if k == 0:
+            pltpu.make_async_copy(srcs[w], outs[w].at[me], loc_sem.at[w]).wait()
+            own(w)
+        elif k == 1: step(w, 1); both(plane, w, 0)
+        elif k == 2: step(w, 2); both(plane, w, 1); both(plane2, w, 0)
+        elif k == 3: step(w, 3); both(plane, w, 2); both(plane2, w, 1)
+        elif k == 4: both(plane, w, 3); both(plane2, w, 2)
+        elif k == 5: both(plane2, w, 3)
+        elif k == 6:
+            for zz in range(4):
+                for xx in range(2):
+                    for yy in range(2):
+                        waitr(w, slab(zz, xx, 1 - c, yy))
+    for t in range(nw + 6):
+        for w in range(nw):
+            k = t - w
+            if 0 <= k <= 6: st(order[w], k)
+    for (w, s, k, d, cond) in pend:
+        if cond is None: cp(w, s, k, d).wait_send()
+        else:
+            @pl.when(cond)
+            def _(): cp(w, s, k, d).wait_send()
+
+def kernel(nw, *refs):
+    srcs = refs[:nw]; outs = refs[nw:2*nw]; send, recv, loc = refs[2*nw:]
+    ag_body(nw, list(range(nw)), srcs, outs, send, recv, loc)
+
+def all_gather(shards, vmem=False):
+    nw = len(shards)
+    if (lax.axis_size("dp"), lax.axis_size("seq")) != (16, 2):
+        return [lax.all_gather(s, ("dp", "seq"), axis=0) for s in shards]
+    sp = pl.BlockSpec(memory_space=pltpu.VMEM if vmem else pl.ANY)
+    return pl.pallas_call(
+        partial(kernel, nw),
+        out_shape=[jax.ShapeDtypeStruct((32,) + s.shape, s.dtype) for s in shards],
+        in_specs=[pl.BlockSpec(memory_space=pl.ANY)] * nw,
+        out_specs=[sp] * nw,
+        scratch_shapes=[pltpu.SemaphoreType.DMA((nw, 36)), pltpu.SemaphoreType.DMA((nw, 32)), pltpu.SemaphoreType.DMA((nw,))],
+        compiler_params=pltpu.CompilerParams(collective_id=0, has_side_effects=True, vmem_limit_bytes=60 * 2**20),
+    )(*shards)
 
 
 EPSILON = 1e-05
@@ -182,15 +315,21 @@
         vectors.astype(jnp.bfloat16),
     )
 
-    def unpack(gathered):
-        qkv_flat, out_flat, up_flat, down_flat, vector_flat = gathered
-        return (
-            qkv_flat.reshape(D, 3 * D),
-            out_flat.reshape(D, D),
-            up_flat.reshape(D, FF),
-            down_flat.reshape(FF, D),
-            vector_flat.astype(jnp.float32),
-        )
+    mine = [
+        shards[0].reshape(-1, 3 * D),
+        shards[1].reshape(-1, D),
+        shards[2].reshape(-1, FF),
+        shards[3].reshape(-1, D),
+        jnp.broadcast_to(jnp.pad(shards[4].astype(jnp.float32), (0, -shards[4].shape[0] % 128))[None], (8, shards[4].shape[0] + -shards[4].shape[0] % 128)),
+    ]
+    full = all_gather(mine)
+    params = (
+        full[0].reshape(D, 3 * D),
+        full[1].reshape(D, D),
+        full[2].reshape(D, FF),
+        full[3].reshape(FF, D),
+        full[4][:, 0, : shards[4].shape[0]].reshape(-1),
+    )
 
     selectors = [head_masks(offsets, branch, HEAD_DIM) for branch in range(3)]
     plans = []
@@ -203,15 +342,6 @@
     layer_rows = []
     grad_rows = []
     for micro_batch in range(MB):
-        params = unpack(
-            (
-                lax.all_gather(shards[0], ("dp", "seq"), axis=0, tiled=True),
-                lax.all_gather(shards[1], ("dp", "seq"), axis=0, tiled=True),
-                lax.all_gather(shards[2], ("dp", "seq"), axis=0, tiled=True),
-                lax.all_gather(shards[3], ("dp", "seq"), axis=0, tiled=True),
-                lax.all_gather(shards[4], ("dp", "seq"), axis=0, tiled=True),
-            )
-        )
         qkv_weight, out_weight, up_weight, down_weight, vector_vals = params
         (
             gain_in,
@@ -287,21 +417,6 @@
         inner_ffn = layer_norm(active, gain_ffn).astype(jnp.bfloat16)
         layer_rows.append(
             (middle + (matmul(inner_ffn, down_weight) + bias_down)).astype(jnp.bfloat16)
-        )
-        back_params = unpack(
-            (
-                lax.all_gather(shards[0], ("dp", "seq"), axis=0, tiled=True),
-                lax.all_gather(shards[1], ("dp", "seq"), axis=0, tiled=True),
-                lax.all_gather(shards[2], ("dp", "seq"), axis=0, tiled=True),
-                lax.all_gather(shards[3], ("dp", "seq"), axis=0, tiled=True),
-                lax.all_gather(shards[4], ("dp", "seq"), axis=0, tiled=True),
-            )
-        )
-        qkv_weight, out_weight, up_weight, down_weight = (
-            back_params[0],
-            back_params[1],
-            back_params[2],
-            back_params[3],
         )
         grad_layer = cotangent[micro_batch, 0].astype(jnp.float32)
         grad_down = grad_layer.astype(jnp.bfloat16)

time: 1100 us -> 1040 us (0.945)
  Pallas kernels: 0 us -> 81.6 us
  waiting for transfers between devices: 441 us -> 379 us
  blocking collectives: 156 us -> 107 us
  local copies, waits for them, and re-layouts: 242 us -> 230 us
    pallas_call x0 -> x1, Pallas kernels: none -> 81.6 us  [all_gather(): pl.pallas_call(partial(kernel, nw), out_shape=[jax.ShapeDtypeStruct((32,)...]
    all_gather x4 -> x0, waiting for transfers between devices: 62.6 us -> none  [the longest x1 59.2 us: per_device(): lax.all_gather(shards[0], ('dp', 'seq'), axis=0, tiled=True)]
    unnamed x2 -> x1, blocking collectives: 81.4 us -> 39.2 us
    reshape x4, local copies, waits for them, and re-layouts: 27.5 us -> 3 us  [the longest x1 0.81 us: per_device(): shards[3].reshape(-1, D)]
    unnamed x480 -> x494, local copies, waits for them, and re-layouts: 24.9 us -> 26.2 us
    unnamed x18 -> x14, waiting for transfers between devices: 378 us -> 379 us
  transfers between devices with their start and end apart: 17 -> 13, of which waited for: 3 -> 1; matrix products, arithmetic and copies ran while one was open for 33% -> 30% of each run, Pallas kernels for 0% -> 0%
where the time goes in v1:
time: 1040 us; the launch traced here: 1030 us
  waiting for transfers between devices  379 us (36%)
  local copies, waits for them, and re-layouts  230 us (22%)
  matrix products  145 us (14%)
  blocking collectives  107 us (10%)
  Pallas kernels  81.6 us (8%)
  other arithmetic  70 us (7%)
  between operations  18 us (2%)
    unnamed x14, waiting for transfers between devices  379 us
    pallas_call x1, Pallas kernels, all_gather(): pl.pallas_call(partial(kernel, nw), out_shape=[jax.ShapeDtypeStruct((32,)...  81.6 us
    unnamed x1, blocking collectives  39.2 us
    dot_general x8, matrix products, outer_sum(): lax.dot_general(left_op, right_op, (((0,), (0,)), ((), ())), preferred_el...  37.2 us
    select_n x28, local copies, waits for them, and re-layouts, spread_rows(): spread = jnp.where(chosen[None], sparse_rows[:, None, :], filler)  33.8 us
    unnamed x494, local copies, waits for them, and re-layouts  26.2 us
    dot_general x8, matrix products, matmul(): return jnp.dot(left_op, right_op, preferred_element_type=jnp.float32)  24.7 us
  transfers between devices with their start and end apart: 13, of which 1 were waited for; matrix products, arithmetic and copies ran while one was open for 30% of the time, Pallas kernels for 0%

profile of v1, /device:TPU:0, one launch (start us, length us, event | category | flops | bytes accessed | tf_op | source)
XLA Modules:
  0.0 1031.2 jit_solution(5150416861775537386)
XLA Ops:
  18.2 81.6 %shard_map.135 = (bf16[32,24,2304]{2,1,0:T(8,128)(2,1)}, bf16[32,24,768]{2,1,0:T(8,128)(2,1)}, bf16[32,24,3072]{2,1,0:T(8,128)(2,1)}, bf16[32,96,768]{2,1,0:T(8,128)(2,1)}, f32[32,8,384]{2,1,0:T(8,128)}) custom-call(bf16[24,2304]{1,0:T(8,128)(2,1)} %reshape.1619.refs_0_, bf16[24,768]{1,0:T(8,128)(2,1)} %reshape.1620.refs_1_, ...), custom_call_target="tpu_custom_call" | custom-call | tf_op jit(solution)/shard_map/pallas_call | solution.py:139
  112.0 5.1 all_gather.38
  118.6 5.0 all_gather.44
  129.5 5.3 all_gather.37
  136.5 5.3 all_gather.43
  144.3 6.5 all_gather.39
  152.7 4.8 all_gather.41
  157.5 4.8 all_gather.47
  162.6 5.4 all_gather.40
  168.3 6.3 all_gather.46
  179.4 6.3 all_gather.36
  186.7 6.3 all_gather.42
  193.9 6.9 all_gather.45
  231.0 6.2 fusion.302
  237.3 6.3 fusion.300
  311.2 3.6 fusion.54
  321.7 3.6 fusion.55
  440.4 3.5 fusion.63
  443.9 3.6 fusion.62
  453.4 5.2 fusion.160
  458.6 5.1 fusion.293
  478.3 4.1 convolution_add_fusion.6
  482.5 9.0 convolution_add_fusion.1
  491.6 5.2 add_bitcast_fusion
  506.7 10.8 %reshape.1676 = f32[2359296]{0:T(1024)} reshape(f32[3072,768]{1,0:T(8,128)} %convolution_add_fusion.1) | data formatting | bytes 18874368 | tf_op jit(solution)/shard_map/reshape | solution.py:536
  517.5 9.6 copy.829
  567.6 3.8 convert_reduce_fusion.8
  572.8 4.1 convolution_add_fusion
  576.9 8.2 reshape.1673
  588.6 4.5 fusion.66
  597.9 39.2 %all-reduce.5 = f32[11520]{0:T(1024)S(1)} all-reduce(f32[11520]{0:T(1024)S(1)} %add.760), channel_id=18, replica_groups=mesh['dp'=16,'seq'=2] {'dp','seq'}, use_global_device_ids=true, to_apply=%region_112.113.clone | all-reduce | flops 11520 | bytes 92160
  639.1 378.6 %all-reduce.9.cloned.1.call-done = (f32[1769472]{0:T(1024)}, f32[589824]{0:T(1024)}, f32[2359296]{0:T(1024)}, f32[2359296]{0:T(1024)}) async-done(((f32[1769472]{0:T(1024)}, f32[589824]{0:T(1024)}, f32[2359296]{0:T(1024)}, f32[2359296]{0:T(1024)}), (f32[1769472]{0:T(1024)}, f32[589824]{0:T(1024)}, f32[2359296]{0:T(1024)}, f32[2359296]{0:T(1024)})) %all-reduce.9.cloned.1.call-update) | async-done | bytes 28311568
  (891 shorter events, 349.4 us)
Async XLA Ops:
  7.2 519.9 %reduce-scatter.37.cloned.1.call-start = ((), (), s32[]{:S(2)}) async-start(), calls=%async_computation.22 | async-start | bytes 147456 | tf_op jit(solution)/shard_map/reduce_scatter | solution.py:485
  8.0 96.0 %copy-start.168 = (pred[12]{0:T(512)(128)(4,1)}, pred[12]{0:T(512)(128)(4,1)S(1)}, u32[]{:S(2)}) copy-start(pred[12]{0:T(512)(128)(4,1)S(1)} %compare_bitcast_fusion) | copy-start | bytes 40
  10.5 92.5 %copy-start = (bf16[2,1,128,768]{3,2,1,0:T(8,128)(2,1)S(1)}, bf16[2,1,128,768]{3,2,1,0:T(8,128)(2,1)}, u32[]{:S(2)}) copy-start(bf16[2,1,128,768]{3,2,1,0:T(8,128)(2,1)} %param.8) | copy-start | bytes 1179652
  117.7 57.3 %copy-start.42 = (f32[12,32,64]{2,1,0:T(8,128)}, f32[12,32,64]{2,1,0:T(8,128)S(1)}, u32[]{:S(2)}) copy-start(f32[12,32,64]{2,1,0:T(8,128)S(1)} %get-tuple-element.257) | copy-start | bytes 294916
  117.9 57.0 %copy-start.107 = (f32[12,32]{1,0:T(8,128)}, f32[12,32]{1,0:T(8,128)S(1)}, u32[]{:S(2)}) copy-start(f32[12,32]{1,0:T(8,128)S(1)} %fusion.261) | copy-start | bytes 4612
  124.2 54.7 %copy-start.43 = (f32[12,32,64]{2,1,0:T(8,128)}, f32[12,32,64]{2,1,0:T(8,128)S(1)}, u32[]{:S(2)}) copy-start(f32[12,32,64]{2,1,0:T(8,128)S(1)} %get-tuple-element.259) | copy-start | bytes 294916
  135.5 66.2 %copy-start.24 = (f32[12,64,64]{1,2,0:T(8,128)}, f32[12,64,64]{1,2,0:T(8,128)S(1)}, u32[]{:S(2)}) copy-start(f32[12,64,64]{1,2,0:T(8,128)S(1)} %get-tuple-element.261) | copy-start | bytes 589828
  135.7 66.0 %copy-start.108 = (f32[12,64]{1,0:T(8,128)}, f32[12,64]{1,0:T(8,128)S(1)}, u32[]{:S(2)}) copy-start(f32[12,64]{1,0:T(8,128)S(1)} %fusion.260) | copy-start | bytes 9220
  142.3 62.1 %copy-start.25 = (f32[12,64,64]{1,2,0:T(8,128)}, f32[12,64,64]{1,2,0:T(8,128)S(1)}, u32[]{:S(2)}) copy-start(f32[12,64,64]{1,2,0:T(8,128)S(1)} %get-tuple-element.263) | copy-start | bytes 589828
  142.4 62.0 %copy-start.110 = (f32[12,64]{1,0:T(8,128)}, f32[12,64]{1,0:T(8,128)S(1)}, u32[]{:S(2)}) copy-start(f32[12,64]{1,0:T(8,128)S(1)} %fusion.263) | copy-start | bytes 9220
  144.3 18.3 %copy-start.89 = (bf16[64,768]{1,0:T(8,128)(2,1)S(1)}, bf16[64,768]{1,0:T(8,128)(2,1)}, u32[]{:S(2)}) copy-start(bf16[64,768]{1,0:T(8,128)(2,1)} %get-tuple-element.100) | copy-start | bytes 294916
  151.1 61.9 %copy-start.40 = (bf16[128,768]{0,1:T(8,128)(2,1)}, bf16[128,768]{0,1:T(8,128)(2,1)S(1)}, u32[]{:S(2)}) copy-start(bf16[128,768]{0,1:T(8,128)(2,1)S(1)} %copy.653) | copy-start | bytes 589828
  151.9 22.9 %copy-start.130 = (f32[32,12]{0,1:T(8,128)S(1)}, f32[32,12]{0,1:T(8,128)}, u32[]{:S(2)}) copy-start(f32[32,12]{0,1:T(8,128)} %fusion.254) | copy-start | bytes 4612
  168.3 33.5 %copy-start.45 = (bf16[64,768]{0,1:T(8,128)(2,1)}, bf16[64,768]{0,1:T(8,128)(2,1)S(1)}, u32[]{:S(2)}) copy-start(bf16[64,768]{0,1:T(8,128)(2,1)S(1)} %copy.655) | copy-start | bytes 294916
  174.8 29.5 %copy-start.44 = (bf16[64,768]{0,1:T(8,128)(2,1)}, bf16[64,768]{0,1:T(8,128)(2,1)S(1)}, u32[]{:S(2)}) copy-start(bf16[64,768]{0,1:T(8,128)(2,1)S(1)} %copy.676) | copy-start | bytes 294916
  273.9 254.6 %reduce-scatter.39.cloned.1.call-start = ((), (), s32[]{:S(2)}) async-start(), calls=%async_computation.23 | async-start | bytes 147456 | tf_op jit(solution)/shard_map/reduce_scatter | solution.py:485
  279.3 250.7 %reduce-scatter.31.cloned.1.call-start = ((), (), s32[]{:S(2)}) async-start(), calls=%async_computation.19 | async-start | bytes 147456 | tf_op jit(solution)/shard_map/reduce_scatter | solution.py:482
  318.4 213.0 %reduce-scatter.21.cloned.1.call-start = ((), (), s32[]{:S(2)}) async-start(), calls=%async_computation.14 | async-start | bytes 147456 | tf_op jit(solution)/shard_map/reduce_scatter | solution.py:482
  328.9 217.4 %reduce-scatter.25.cloned.1.call-start = ((), (), s32[]{:S(2)}) async-start(), calls=%async_computation.16 | async-start | bytes 294912 | tf_op jit(solution)/shard_map/reduce_scatter | solution.py:479
  355.9 192.0 %reduce-scatter.35.cloned.1.call-start = ((), (), s32[]{:S(2)}) async-start(), calls=%async_computation.21 | async-start | bytes 294912 | tf_op jit(solution)/shard_map/reduce_scatter | solution.py:479
  363.8 185.7 %reduce-scatter.19.cloned.1.call-start = ((), (), s32[]{:S(2)}) async-start(), calls=%async_computation.13 | async-start | bytes 294912 | tf_op jit(solution)/shard_map/reduce_scatter | solution.py:476
  377.8 173.3 %reduce-scatter.29.cloned.1.call-start = ((), (), s32[]{:S(2)}) async-start(), calls=%async_computation.18 | async-start | bytes 294912 | tf_op jit(solution)/shard_map/reduce_scatter | solution.py:476
  389.7 177.8 %reduce-scatter.33.cloned.1.call-start = ((), (), s32[]{:S(2)}) async-start(), calls=%async_computation.20 | async-start | bytes 589824 | tf_op jit(solution)/shard_map/reduce_scatter | solution.py:473
  398.3 169.2 %reduce-scatter.23.cloned.1.call-start = ((), (), s32[]{:S(2)}) async-start(), calls=%async_computation.15 | async-start | bytes 589824 | tf_op jit(solution)/shard_map/reduce_scatter | solution.py:473
  406.8 160.7 %reduce-scatter.17.cloned.1.call-start = ((), (), s32[]{:S(2)}) async-start(), calls=%async_computation.12 | async-start | bytes 589824 | tf_op jit(solution)/shard_map/reduce_scatter | solution.py:470
  424.2 143.3 %reduce-scatter.27.cloned.1.call-start = ((), (), s32[]{:S(2)}) async-start(), calls=%async_computation.17 | async-start | bytes 589824 | tf_op jit(solution)/shard_map/reduce_scatter | solution.py:470
  434.0 583.7 %all-reduce.9.cloned.1.call-start = ((), (), s32[]{:S(2)}) async-start(), calls=%async_computation.24 | async-start | bytes 56623104
  596.9 40.9 %copy-start.33 = (bf16[2,1,128,768]{3,2,1,0:T(8,128)(2,1)S(1)}, bf16[2,1,128,768]{3,2,1,0:T(8,128)(2,1)}, u32[]{:S(2)}) copy-start(bf16[2,1,128,768]{3,2,1,0:T(8,128)(2,1)} %param.9) | copy-start | bytes 1179652
  596.9 40.9 %copy-start.36 = (f32[128,768]{1,0:T(8,128)S(1)}, f32[128,768]{1,0:T(8,128)}, u32[]{:S(2)}) copy-start(f32[128,768]{1,0:T(8,128)} %copy-done.35) | copy-start | bytes 1179652
  596.9 40.9 %copy-start.38 = (f32[128,768]{1,0:T(8,128)S(1)}, f32[128,768]{1,0:T(8,128)}, u32[]{:S(2)}) copy-start(f32[128,768]{1,0:T(8,128)} %copy-done.37) | copy-start | bytes 1179652
  596.9 40.9 %copy-start.205 = (f32[128]{0:T(128)S(1)}, f32[128]{0:T(128)}, u32[]{:S(2)}) copy-start(f32[128]{0:T(128)} %copy-done.204) | copy-start | bytes 1540
  596.9 40.9 %copy-start.207 = (f32[128]{0:T(128)S(1)}, f32[128]{0:T(128)}, u32[]{:S(2)}) copy-start(f32[128]{0:T(128)} %copy-done.206) | copy-start | bytes 1540
  (214 other events, 852.1 us)
Sparse Core Ops, SparseCore 0:
  274.0 9.2 reduce-scatter.36
  285.5 9.9 reduce-scatter.38
  318.5 9.2 reduce-scatter.30
  329.8 9.9 reduce-scatter.20
  356.0 10.1 reduce-scatter.24
  368.3 10.9 reduce-scatter.34
  381.5 10.9 reduce-scatter.18
  394.8 10.9 reduce-scatter.28
  408.0 13.1 reduce-scatter.32
  423.4 13.1 reduce-scatter.22
  438.8 13.0 reduce-scatter.16
  454.1 13.1 reduce-scatter.26
  585.2 432.4 all-reduce.8
